TPU v7x, 256 devices: a whole 4x4x8 slice. The times are simulated.
256 devices in a mesh: slab: 32 (over y, z), mode: 8 (over x, core).
Axes of the slice: x: 4, y: 4, z: 8, core: 2. Of those that a mesh axis runs over, the one named last changes fastest.
Arguments:
- positions: float32 [3, 524288], P(None, ('slab', 'mode')), may hold values from 0 to 1, as said below
- charges: float32 [524288], P(('slab', 'mode')), may hold values from -0.03125 to 0.03125
- counts: int32 [32], replicated, may hold values from 3840 to 16384, as said below
- box: float32 [2], replicated, may hold values from 0.8 to 1.25
Outputs:
- forces: float32 [3, 524288], P(None, ('slab', 'mode'))
Inputs may be any that keep to these rules, and one draw needn't show every extreme that they name: positions[0] and positions[1] are fractional coordinates; positions[2, i] lies strictly between s 0.08 / 32 and (s + 1) 0.08 / 32 for s = i // 16384, and never falls with i within a slab. The live ions of a slab are its first counts[s] slots; some slab is full.
All inputs are finite; a program needn't handle non-finite values.
Results may differ from a plain program's by a relative error of at most 0.0003.
Values sent between devices are 32-bit elements; how exact they have to be, the bound alone decides.
A program may use at most 64 MiB of HBM per device.

v0:
```python
import math

import jax
import jax.numpy as jnp
from jax import lax
from jax.sharding import PartitionSpec as P

QDIM = 64
BLOCK = 512
MODES = 4096


two_pi = 2.0 * math.pi
slab_span = 0.08


def carried_in(value, axis, combine, identity, reverse):
    size, mine = (lax.axis_size(axis), lax.axis_index(axis))
    everything = jax.tree.map(lambda part: lax.all_gather(part, axis), value)
    start = jax.tree.map(
        lambda part, zero: jnp.broadcast_to(jnp.asarray(zero, part.dtype), part.shape),
        value,
        identity,
    )

    def lap(k, before):
        at = size - 1 - k if reverse else k
        reached = at > mine if reverse else at < mine
        new = combine(before, jax.tree.map(lambda part: part[at], everything))
        return jax.tree.map(lambda a, b: jnp.where(reached, a, b), new, before)

    return lax.fori_loop(0, size, lap, start)


def wave_table(first_mode, mode_count, box):
    mode_index = first_mode + jnp.arange(mode_count, dtype=jnp.int32)
    order_p = (mode_index // QDIM + 1).astype(jnp.float32)
    order_q = (mode_index % QDIM - QDIM // 2).astype(jnp.float32)
    wave_x = two_pi * order_p / box[0]
    wave_y = two_pi * order_q / box[1]
    wave_norm = jnp.sqrt(wave_x * wave_x + wave_y * wave_y)
    return (order_p, order_q, wave_x / wave_norm, wave_y / wave_norm, wave_norm)


def phase_terms(mode_info, coords, lower_edge, height):
    order_p, order_q, unit_x, unit_y, wave_norm = mode_info
    phase_angle = two_pi * (
        order_p[:, None] * coords[0][None, :] + order_q[:, None] * coords[1][None, :]
    )
    ion_depth = coords[2][None, :] - lower_edge
    e_low = jnp.exp(-wave_norm[:, None] * ion_depth)
    e_high = jnp.exp(-wave_norm[:, None] * (height - ion_depth))
    return (jnp.cos(phase_angle), jnp.sin(phase_angle), e_low, e_high)


def block_moments(mode_info, coords, weight, lower_edge, height):
    cosine, sine_part, e_low, e_high = phase_terms(mode_info, coords, lower_edge, height)
    upward = weight[None, :] * e_high
    downward = weight[None, :] * e_low
    row_stack = jnp.stack(
        [upward * cosine, upward * sine_part, downward * cosine, downward * sine_part]
    )
    mode_count = cosine.shape[0]
    return jnp.sum(row_stack.reshape(4, mode_count, cosine.shape[1] // BLOCK, BLOCK), axis=3)


def force_terms(mode_info, coords, weight, coefficients, lower_edge, height, box):
    order_p, order_q, unit_x, unit_y, wave_norm = mode_info
    cosine, sine_part, e_low, e_high = phase_terms(mode_info, coords, lower_edge, height)
    mode_count, ion_count = cosine.shape
    block_count = coefficients.shape[2]

    def spread(row_values):
        return jnp.broadcast_to(row_values[:, :, None], (mode_count, block_count, BLOCK)).reshape(
            mode_count, ion_count
        )

    below_c = e_low * spread(coefficients[0])
    below_s = e_low * spread(coefficients[1])
    above_c = e_high * spread(coefficients[2])
    above_s = e_high * spread(coefficients[3])
    in_plane = sine_part * (below_c + above_c) - cosine * (below_s + above_s)
    normal = cosine * (below_c - above_c) + sine_part * (below_s - above_s)
    scale = 2.0 * two_pi / (box[0] * box[1]) * weight
    return (
        jnp.stack(
            [
                jnp.sum(unit_x[:, None] * in_plane, axis=0),
                jnp.sum(unit_y[:, None] * in_plane, axis=0),
                jnp.sum(normal, axis=0),
            ]
        )
        * scale[None, :]
    )


def group_blocks(ion_total):
    block_count = ion_total // BLOCK
    chosen = 1
    for factor in range(1, 5):
        if block_count % factor == 0:
            chosen = factor
    return chosen


def sweep_moments(mode_info, coords, weight, lower_edge, height):
    ion_total = coords.shape[1]
    per_group = group_blocks(ion_total)
    group_width = per_group * BLOCK
    group_count = ion_total // group_width
    coord_groups = coords.reshape(3, group_count, group_width).transpose(1, 0, 2)
    weight_groups = weight.reshape(group_count, group_width)

    def advance(carried, group_item):
        return (carried, block_moments(mode_info, group_item[0], group_item[1], lower_edge, height))

    _, pieces = lax.scan(advance, jnp.int32(0), (coord_groups, weight_groups))
    mode_count = pieces.shape[2]
    return pieces.transpose(1, 2, 0, 3).reshape(4, mode_count, group_count * per_group)


def sweep_forces(mode_info, coords, weight, coefficients, lower_edge, height, box):
    ion_total = coords.shape[1]
    per_group = group_blocks(ion_total)
    group_width = per_group * BLOCK
    group_count = ion_total // group_width
    mode_count = coefficients.shape[1]
    coord_groups = coords.reshape(3, group_count, group_width).transpose(1, 0, 2)
    weight_groups = weight.reshape(group_count, group_width)
    coeff_groups = coefficients.reshape(4, mode_count, group_count, per_group).transpose(2, 0, 1, 3)

    def advance(carried, group_item):
        return (
            carried,
            force_terms(
                mode_info, group_item[0], group_item[1], group_item[2], lower_edge, height, box
            ),
        )

    _, pieces = lax.scan(advance, jnp.int32(0), (coord_groups, weight_groups, coeff_groups))
    return pieces.transpose(1, 0, 2).reshape(3, ion_total)


def carry_coefficients(moments, wave_norm, height):
    mode_count = moments.shape[1]
    block_count = moments.shape[2]
    block_ids = jnp.arange(block_count, dtype=jnp.int32)
    lower_tri = (block_ids[:, None] < block_ids[None, :]).astype(jnp.float32)
    upper_tri = (block_ids[:, None] > block_ids[None, :]).astype(jnp.float32)
    prefix_up = jnp.dot(
        moments[0:2].reshape(2 * mode_count, block_count),
        lower_tri,
        precision=lax.Precision.HIGHEST,
    ).reshape(2, mode_count, block_count)
    suffix_down = jnp.dot(
        moments[2:4].reshape(2 * mode_count, block_count),
        upper_tri,
        precision=lax.Precision.HIGHEST,
    ).reshape(2, mode_count, block_count)
    totals = jnp.sum(moments, axis=2)
    decay_step = jnp.exp(-wave_norm * height)

    def compose(earlier, later):
        return (earlier[0] * later[0], earlier[1] * later[0][None, :] + later[1])

    identity = (jnp.ones_like(decay_step), jnp.zeros((2, mode_count), jnp.float32))
    _, carry_up = carried_in((decay_step, totals[0:2]), "slab", compose, identity, False)
    _, carry_down = carried_in((decay_step, totals[2:4]), "slab", compose, identity, True)
    boost_step = jnp.exp(wave_norm * height)[None, :, None]
    return jnp.concatenate(
        [
            carry_up[:, :, None] + boost_step * prefix_up,
            carry_down[:, :, None] + boost_step * suffix_down,
        ],
        axis=0,
    )


def shards(positions, charges, counts, box):
    slab_count = lax.axis_size("slab")
    mode_parts = lax.axis_size("mode")
    slab_rank = lax.axis_index("slab")
    mode_rank = lax.axis_index("mode")
    modes_dev = MODES // mode_parts
    height = slab_span / slab_count
    lower_edge = slab_rank.astype(jnp.float32) * height
    live_count = jnp.sum(jnp.where(jnp.arange(slab_count, dtype=jnp.int32) == slab_rank, counts, 0))
    coords, charge = (
        lax.all_gather(positions, "mode", axis=1, tiled=True),
        lax.all_gather(charges, "mode", axis=0, tiled=True),
    )
    live_mask = jnp.arange(coords.shape[1], dtype=jnp.int32) < live_count
    weight = jnp.where(live_mask, charge, jnp.float32(0.0))
    mode_info = wave_table(mode_rank * modes_dev, modes_dev, box)
    moments = sweep_moments(mode_info, coords, weight, lower_edge, height)
    coefficients = carry_coefficients(moments, mode_info[4], height)
    partial_force = sweep_forces(mode_info, coords, weight, coefficients, lower_edge, height, box)
    return lax.psum_scatter(partial_force, "mode", scatter_dimension=1, tiled=True)


def solution(mesh):
    return jax.shard_map(
        shards,
        mesh=mesh,
        in_specs=(P(None, ("slab", "mode")), P(("slab", "mode")), P(), P()),
        out_specs=P(None, ("slab", "mode")),
        check_vma=False,
    )
```

profile of v0, /device:TPU:1, one launch (start us, length us, event | category | flops | bytes accessed | tf_op | source)
XLA Modules:
  0.0 587.2 jit_solution(16965568512662683384)
XLA Ops:
  6.5 1.4 fusion.79
  7.9 1.3 exponential_bitcast_fusion
  11.8 1.4 fusion.77
  13.1 16.0 %all_gather.26 = f32[16384]{0:T(1024)S(1)} all-gather(f32[2048]{0:T(1024)} %param.13), channel_id=1, replica_groups=mesh['slab'=32,'mode'=8] {'mode'}, dimensions={0}, use_global_device_ids=true | all-gather | bytes 73728 | tf_op jit(solution)/shard_map/all_gather | solution.py:190
  29.8 13.1 %all_gather.24 = f32[3,16384]{1,0:T(4,128)S(1)} all-gather(f32[3,2048]{1,0:T(4,128)} %param.12), channel_id=1, replica_groups=mesh['slab'=32,'mode'=8] {'mode'}, dimensions={1}, use_global_device_ids=true | all-gather | bytes 221184 | tf_op jit(solution)/shard_map/all_gather | solution.py:189
  42.9 161.3 %while.60 = (s32[]{:T(128)}, f32[8,4,512,4]{2,3,1,0:T(4,128)S(1)}, f32[8,2048]{1,0:T(8,128)S(1)}, f32[8,3,2048]{2,1,0:T(4,128)S(1)}, f32[]{:T(128)}, /*index=5*/...) while((s32[]{:T(128)}, f32[8,4,512,4]{2,3,1,0:T(4,128)S(1)}, ...), condition=%wide.region_3.4_spmd.clone.clone, body=%wide.region_1.3_spmd.clone.clone.sunk | while | flops 29384708 | bytes 33853620 | solution.py:117
  43.0 1.3 sqrt_negate_fusion.4
  44.3 17.2 %fusion.91 = (f32[1,512,4,512]{3,1,2,0:T(8,128)S(1)}, f32[1,512,4,512]{3,1,2,0:T(8,128)S(1)}, f32[1,512,4,512]{3,1,2,0:T(8,128)S(1)}, f32[1,512,4,512]{3,1,2,0:T(8,128)S(1)}) fusion(f32[4,512]{1,0:T(4,128)S(1)} %mul.1380, f32[512]{0:T(512)S(1)} %get-tuple-element.909, f32[4,512]{1,0:T(4,128)S(1)} %mul.1381, f32[512]{0:T(512)S(1)} %get-tuple-element.911, ...), kind=kLoop, calls=%fused_computation.21.clone.1 | loop fusion | flops 12582912 | bytes 16824320 | tf_op jit(solution)/shard_map/while/body/eval_jaxpr/mul | solution.py:61
  61.5 1.4 maximum_reduce_fusion.2
  64.5 17.2 %fusion.91 = (f32[1,512,4,512]{3,1,2,0:T(8,128)S(1)}, f32[1,512,4,512]{3,1,2,0:T(8,128)S(1)}, f32[1,512,4,512]{3,1,2,0:T(8,128)S(1)}, f32[1,512,4,512]{3,1,2,0:T(8,128)S(1)}) fusion(f32[4,512]{1,0:T(4,128)S(1)} %mul.1380, f32[512]{0:T(512)S(1)} %get-tuple-element.909, f32[4,512]{1,0:T(4,128)S(1)} %mul.1381, f32[512]{0:T(512)S(1)} %get-tuple-element.911, ...), kind=kLoop, calls=%fused_computation.21.clone.1 | loop fusion | flops 12582912 | bytes 16824320 | tf_op jit(solution)/shard_map/while/body/eval_jaxpr/mul | solution.py:61
  81.7 1.4 maximum_reduce_fusion.2
  84.7 17.2 %fusion.91 = (f32[1,512,4,512]{3,1,2,0:T(8,128)S(1)}, f32[1,512,4,512]{3,1,2,0:T(8,128)S(1)}, f32[1,512,4,512]{3,1,2,0:T(8,128)S(1)}, f32[1,512,4,512]{3,1,2,0:T(8,128)S(1)}) fusion(f32[4,512]{1,0:T(4,128)S(1)} %mul.1380, f32[512]{0:T(512)S(1)} %get-tuple-element.909, f32[4,512]{1,0:T(4,128)S(1)} %mul.1381, f32[512]{0:T(512)S(1)} %get-tuple-element.911, ...), kind=kLoop, calls=%fused_computation.21.clone.1 | loop fusion | flops 12582912 | bytes 16824320 | tf_op jit(solution)/shard_map/while/body/eval_jaxpr/mul | solution.py:61
  101.9 1.4 maximum_reduce_fusion.2
  104.8 17.2 %fusion.91 = (f32[1,512,4,512]{3,1,2,0:T(8,128)S(1)}, f32[1,512,4,512]{3,1,2,0:T(8,128)S(1)}, f32[1,512,4,512]{3,1,2,0:T(8,128)S(1)}, f32[1,512,4,512]{3,1,2,0:T(8,128)S(1)}) fusion(f32[4,512]{1,0:T(4,128)S(1)} %mul.1380, f32[512]{0:T(512)S(1)} %get-tuple-element.909, f32[4,512]{1,0:T(4,128)S(1)} %mul.1381, f32[512]{0:T(512)S(1)} %get-tuple-element.911, ...), kind=kLoop, calls=%fused_computation.21.clone.1 | loop fusion | flops 12582912 | bytes 16824320 | tf_op jit(solution)/shard_map/while/body/eval_jaxpr/mul | solution.py:61
  122.0 1.4 maximum_reduce_fusion.2
  125.0 17.2 %fusion.91 = (f32[1,512,4,512]{3,1,2,0:T(8,128)S(1)}, f32[1,512,4,512]{3,1,2,0:T(8,128)S(1)}, f32[1,512,4,512]{3,1,2,0:T(8,128)S(1)}, f32[1,512,4,512]{3,1,2,0:T(8,128)S(1)}) fusion(f32[4,512]{1,0:T(4,128)S(1)} %mul.1380, f32[512]{0:T(512)S(1)} %get-tuple-element.909, f32[4,512]{1,0:T(4,128)S(1)} %mul.1381, f32[512]{0:T(512)S(1)} %get-tuple-element.911, ...), kind=kLoop, calls=%fused_computation.21.clone.1 | loop fusion | flops 12582912 | bytes 16824320 | tf_op jit(solution)/shard_map/while/body/eval_jaxpr/mul | solution.py:61
  142.2 1.4 maximum_reduce_fusion.2
  145.2 17.2 %fusion.91 = (f32[1,512,4,512]{3,1,2,0:T(8,128)S(1)}, f32[1,512,4,512]{3,1,2,0:T(8,128)S(1)}, f32[1,512,4,512]{3,1,2,0:T(8,128)S(1)}, f32[1,512,4,512]{3,1,2,0:T(8,128)S(1)}) fusion(f32[4,512]{1,0:T(4,128)S(1)} %mul.1380, f32[512]{0:T(512)S(1)} %get-tuple-element.909, f32[4,512]{1,0:T(4,128)S(1)} %mul.1381, f32[512]{0:T(512)S(1)} %get-tuple-element.911, ...), kind=kLoop, calls=%fused_computation.21.clone.1 | loop fusion | flops 12582912 | bytes 16824320 | tf_op jit(solution)/shard_map/while/body/eval_jaxpr/mul | solution.py:61
  162.3 1.4 maximum_reduce_fusion.2
  165.3 17.2 %fusion.91 = (f32[1,512,4,512]{3,1,2,0:T(8,128)S(1)}, f32[1,512,4,512]{3,1,2,0:T(8,128)S(1)}, f32[1,512,4,512]{3,1,2,0:T(8,128)S(1)}, f32[1,512,4,512]{3,1,2,0:T(8,128)S(1)}) fusion(f32[4,512]{1,0:T(4,128)S(1)} %mul.1380, f32[512]{0:T(512)S(1)} %get-tuple-element.909, f32[4,512]{1,0:T(4,128)S(1)} %mul.1381, f32[512]{0:T(512)S(1)} %get-tuple-element.911, ...), kind=kLoop, calls=%fused_computation.21.clone.1 | loop fusion | flops 12582912 | bytes 16824320 | tf_op jit(solution)/shard_map/while/body/eval_jaxpr/mul | solution.py:61
  182.5 1.4 maximum_reduce_fusion.2
  185.5 17.2 %fusion.91 = (f32[1,512,4,512]{3,1,2,0:T(8,128)S(1)}, f32[1,512,4,512]{3,1,2,0:T(8,128)S(1)}, f32[1,512,4,512]{3,1,2,0:T(8,128)S(1)}, f32[1,512,4,512]{3,1,2,0:T(8,128)S(1)}) fusion(f32[4,512]{1,0:T(4,128)S(1)} %mul.1380, f32[512]{0:T(512)S(1)} %get-tuple-element.909, f32[4,512]{1,0:T(4,128)S(1)} %mul.1381, f32[512]{0:T(512)S(1)} %get-tuple-element.911, ...), kind=kLoop, calls=%fused_computation.21.clone.1 | loop fusion | flops 12582912 | bytes 16824320 | tf_op jit(solution)/shard_map/while/body/eval_jaxpr/mul | solution.py:61
  202.7 1.4 maximum_reduce_fusion.2
  204.2 35.3 %all-gather.3 = f32[32,2,512]{2,1,0:T(2,128)S(1)} all-gather(f32[1,2,512]{2,1,0:T(2,128)S(1)} %get-tuple-element.719), channel_id=2, replica_groups=mesh['slab'=32,'mode'=8] {'slab'}, dimensions={0}, use_global_device_ids=true | all-gather | bytes 135168 | tf_op jit(solution)/shard_map/all_gather | solution.py:19
  239.6 36.0 %all-gather.2 = f32[32,1,512]{2,1,0:T(1,128)S(1)} all-gather(f32[1,1,512]{2,1,0:T(1,128)S(1)} %exponential_bitcast_fusion), channel_id=1, replica_groups=mesh['slab'=32,'mode'=8] {'slab'}, dimensions={0}, use_global_device_ids=true | all-gather | bytes 67584 | tf_op jit(solution)/shard_map/all_gather | solution.py:19
  275.5 1.9 while.58
  277.5 31.4 %all-gather.4 = f32[32,2,512]{2,1,0:T(2,128)S(1)} all-gather(f32[1,2,512]{2,1,0:T(2,128)S(1)} %get-tuple-element.720), channel_id=3, replica_groups=mesh['slab'=32,'mode'=8] {'slab'}, dimensions={0}, use_global_device_ids=true | all-gather | bytes 135168 | tf_op jit(solution)/shard_map/all_gather | solution.py:19
  308.9 2.3 while.59
  311.8 178.5 %while.61 = (s32[]{:T(128)}, f32[8,3,2048]{2,1,0:T(4,128)S(1)}, f32[8,3,2048]{2,1,0:T(4,128)S(1)}, f32[]{:T(128)}, f32[8,4,512,4]{2,3,1,0:T(4,128)S(1)}, /*index...) while((s32[]{:T(128)}, f32[8,3,2048]{2,1,0:T(4,128)S(1)}, ...), condition=%wide.region_13.14_spmd.clone.clone, body=%wide.region_9.13_spmd.clone.clone.sunk | while | flops 26279428 | bytes 422137 | solution.py:140
  313.3 1.3 sqrt_negate_fusion.5
  314.6 19.4 %multiply_reduce_fusion.3 = (f32[4,512]{1,0:T(4,128)S(1)}, f32[4,512]{1,0:T(4,128)S(1)}, f32[4,512]{1,0:T(4,128)S(1)}) fusion(f32[512,4]{0,1:T(4,128)S(1)} %get-tuple-element.927, f32[512,4]{0,1:T(4,128)S(1)} %get-tuple-element.928, f32[512,4]{0,1:T(4,128)S(1)} %get-tuple-element.929, f32[4,512]{1,0:T(4,128)S(1)} %broadcast_subtract_fusion.5, ...), kind=kLoop, calls=%fused_computation.59.clone.1 | loop fusion | flops 26208256 | bytes 100352 | tf_op jit(solution)/shard_map/while/body/eval_jaxpr/reduce_sum | solution.py:88
  335.6 1.3 sqrt_negate_fusion.5
  336.9 19.4 %multiply_reduce_fusion.3 = (f32[4,512]{1,0:T(4,128)S(1)}, f32[4,512]{1,0:T(4,128)S(1)}, f32[4,512]{1,0:T(4,128)S(1)}) fusion(f32[512,4]{0,1:T(4,128)S(1)} %get-tuple-element.927, f32[512,4]{0,1:T(4,128)S(1)} %get-tuple-element.928, f32[512,4]{0,1:T(4,128)S(1)} %get-tuple-element.929, f32[4,512]{1,0:T(4,128)S(1)} %broadcast_subtract_fusion.5, ...), kind=kLoop, calls=%fused_computation.59.clone.1 | loop fusion | flops 26208256 | bytes 100352 | tf_op jit(solution)/shard_map/while/body/eval_jaxpr/reduce_sum | solution.py:88
  357.9 1.3 sqrt_negate_fusion.5
  359.2 19.4 %multiply_reduce_fusion.3 = (f32[4,512]{1,0:T(4,128)S(1)}, f32[4,512]{1,0:T(4,128)S(1)}, f32[4,512]{1,0:T(4,128)S(1)}) fusion(f32[512,4]{0,1:T(4,128)S(1)} %get-tuple-element.927, f32[512,4]{0,1:T(4,128)S(1)} %get-tuple-element.928, f32[512,4]{0,1:T(4,128)S(1)} %get-tuple-element.929, f32[4,512]{1,0:T(4,128)S(1)} %broadcast_subtract_fusion.5, ...), kind=kLoop, calls=%fused_computation.59.clone.1 | loop fusion | flops 26208256 | bytes 100352 | tf_op jit(solution)/shard_map/while/body/eval_jaxpr/reduce_sum | solution.py:88
  380.2 1.3 sqrt_negate_fusion.5
  381.5 19.4 %multiply_reduce_fusion.3 = (f32[4,512]{1,0:T(4,128)S(1)}, f32[4,512]{1,0:T(4,128)S(1)}, f32[4,512]{1,0:T(4,128)S(1)}) fusion(f32[512,4]{0,1:T(4,128)S(1)} %get-tuple-element.927, f32[512,4]{0,1:T(4,128)S(1)} %get-tuple-element.928, f32[512,4]{0,1:T(4,128)S(1)} %get-tuple-element.929, f32[4,512]{1,0:T(4,128)S(1)} %broadcast_subtract_fusion.5, ...), kind=kLoop, calls=%fused_computation.59.clone.1 | loop fusion | flops 26208256 | bytes 100352 | tf_op jit(solution)/shard_map/while/body/eval_jaxpr/reduce_sum | solution.py:88
  402.5 1.3 sqrt_negate_fusion.5
  403.8 19.4 %multiply_reduce_fusion.3 = (f32[4,512]{1,0:T(4,128)S(1)}, f32[4,512]{1,0:T(4,128)S(1)}, f32[4,512]{1,0:T(4,128)S(1)}) fusion(f32[512,4]{0,1:T(4,128)S(1)} %get-tuple-element.927, f32[512,4]{0,1:T(4,128)S(1)} %get-tuple-element.928, f32[512,4]{0,1:T(4,128)S(1)} %get-tuple-element.929, f32[4,512]{1,0:T(4,128)S(1)} %broadcast_subtract_fusion.5, ...), kind=kLoop, calls=%fused_computation.59.clone.1 | loop fusion | flops 26208256 | bytes 100352 | tf_op jit(solution)/shard_map/while/body/eval_jaxpr/reduce_sum | solution.py:88
  424.8 1.3 sqrt_negate_fusion.5
  426.2 19.4 %multiply_reduce_fusion.3 = (f32[4,512]{1,0:T(4,128)S(1)}, f32[4,512]{1,0:T(4,128)S(1)}, f32[4,512]{1,0:T(4,128)S(1)}) fusion(f32[512,4]{0,1:T(4,128)S(1)} %get-tuple-element.927, f32[512,4]{0,1:T(4,128)S(1)} %get-tuple-element.928, f32[512,4]{0,1:T(4,128)S(1)} %get-tuple-element.929, f32[4,512]{1,0:T(4,128)S(1)} %broadcast_subtract_fusion.5, ...), kind=kLoop, calls=%fused_computation.59.clone.1 | loop fusion | flops 26208256 | bytes 100352 | tf_op jit(solution)/shard_map/while/body/eval_jaxpr/reduce_sum | solution.py:88
  447.1 1.3 sqrt_negate_fusion.5
  448.5 19.4 %multiply_reduce_fusion.3 = (f32[4,512]{1,0:T(4,128)S(1)}, f32[4,512]{1,0:T(4,128)S(1)}, f32[4,512]{1,0:T(4,128)S(1)}) fusion(f32[512,4]{0,1:T(4,128)S(1)} %get-tuple-element.927, f32[512,4]{0,1:T(4,128)S(1)} %get-tuple-element.928, f32[512,4]{0,1:T(4,128)S(1)} %get-tuple-element.929, f32[4,512]{1,0:T(4,128)S(1)} %broadcast_subtract_fusion.5, ...), kind=kLoop, calls=%fused_computation.59.clone.1 | loop fusion | flops 26208256 | bytes 100352 | tf_op jit(solution)/shard_map/while/body/eval_jaxpr/reduce_sum | solution.py:88
  469.5 1.3 sqrt_negate_fusion.5
  470.8 19.4 %multiply_reduce_fusion.3 = (f32[4,512]{1,0:T(4,128)S(1)}, f32[4,512]{1,0:T(4,128)S(1)}, f32[4,512]{1,0:T(4,128)S(1)}) fusion(f32[512,4]{0,1:T(4,128)S(1)} %get-tuple-element.927, f32[512,4]{0,1:T(4,128)S(1)} %get-tuple-element.928, f32[512,4]{0,1:T(4,128)S(1)} %get-tuple-element.929, f32[4,512]{1,0:T(4,128)S(1)} %broadcast_subtract_fusion.5, ...), kind=kLoop, calls=%fused_computation.59.clone.1 | loop fusion | flops 26208256 | bytes 100352 | tf_op jit(solution)/shard_map/while/body/eval_jaxpr/reduce_sum | solution.py:88
  490.3 5.1 copy.33
  495.4 82.8 %reduce-scatter.4.cloned.1.call-done = f32[2048,3]{1,0:T(8,128)} async-done(((f32[16384,3]{1,0:T(8,128)}), f32[2048,3]{1,0:T(8,128)}) %reduce-scatter.4.cloned.1.call-update) | async-done | bytes 24592
  578.2 2.2 copy.34
  (333 shorter events, 27.2 us)
Async XLA Ops:
  6.5 571.7 %reduce-scatter.4.cloned.1.call-start = ((), (), s32[]{:S(2)}) async-start(), calls=%async_computation.1 | async-start | bytes 9437184
Sparse Core Ops, SparseCore 0:
  495.6 82.6 reduce-scatter.3
where the time goes:
time: 588 us; the launch traced here: 587 us
  other arithmetic  343 us (58%)
  blocking collectives  132 us (22%)
  waiting for transfers between devices  82.8 us (14%)
  between operations  14.9 us (3%)
  local copies, waits for them, and re-layouts  11.1 us (2%)
    reduce_sum x8, other arithmetic, force_terms(): jnp.sum(unit_x[:, None] * in_plane, axis=0)  155 us
    mul x8, other arithmetic, block_moments(): upward * cosine  137 us
    all_gather x3, blocking collectives, carried_in(): everything = jax.tree.map(lambda part: lax.all_gather(part, axis), value)  103 us
    unnamed x2, waiting for transfers between devices  82.8 us
    neg x16, other arithmetic, phase_terms(): e_high = jnp.exp(-wave_norm[:, None] * (height - ion_depth))  20.6 us
    all_gather x1, blocking collectives, shards(): lax.all_gather(charges, 'mode', axis=0, tiled=True)  16 us
    all_gather x1, blocking collectives, shards(): lax.all_gather(positions, 'mode', axis=1, tiled=True)  13.1 us
  transfers between devices with their start and end apart: 1, of which 1 were waited for; matrix products, arithmetic and copies ran while one was open for 0% of the time, Pallas kernels for 0%

commit v1 on v0

v1 whole, which is shorter than its diff:
```python
import math

import jax
import jax.numpy as jnp
from jax import lax
from jax.experimental import pallas as pl
from jax.experimental.pallas import tpu as pltpu
from jax.sharding import PartitionSpec as P

BLOCK = 512
SLABS = 32
GROUP = 8
OWN = 2048
BLOCKS = OWN // BLOCK
SPAN = 0.08
TWO_PI = 2.0 * math.pi
F32 = jnp.float32
BF16 = jnp.bfloat16

EXP = (
    0.999999988350913, 0.9999999941834263, 0.5000007545561663, 0.16666682366413116,
    0.04165903378572252, 0.008332189708132568, 0.001413565070950797, 0.0002014945763397459,
)
COS = (
    0.9999999890590228, -19.73920449945383, 64.93911745989081, -85.45013953079767,
    60.167630950263465, -25.967599245923743, 6.52865815775625,
)
SIN = (
    6.283185302511503, -41.34170040531721, 81.6051313857832, -76.70301535364747,
    42.02592698447418, -14.899846663536497, 3.2381375046186873,
)
POWERS = 8

LOW = 64 * POWERS
EXTRA = LOW + 64 * 3
ROWS = EXTRA + 64


def horner(coefs, z):
    acc = coefs[-1] * z + coefs[-2]
    for c in coefs[-3::-1]:
        acc = acc * z + c
    return acc


def frac(t):
    return t - jnp.round(t)


def cos_turn(r):
    return horner(COS, r * r)


def sin_turn(r):
    return r * horner(SIN, r * r)


def iota(shape, dim):
    return lax.broadcasted_iota(jnp.int32, shape, dim)


def split(v):
    hi = v.astype(BF16)
    return hi, (v - hi.astype(F32)).astype(BF16)


def y_order(index):
    order = jnp.where(index < 32, index, jnp.where(index == 32, 32, index - 32))
    return order.astype(F32)


def waves(order_p, order_q, box0, box1):
    wave_x = TWO_PI * order_p / box0
    wave_y = TWO_PI * order_q / box1
    return wave_x, wave_y, jnp.sqrt(wave_x * wave_x + wave_y * wave_y)


def turn(row):
    return pltpu.roll(row, 64, 1)


def kernel(
    counts, box, pos, chg, out,
    tf, e_ref, we, stack, tab, tab32, up, down, total, rx1, sums, rx2, tx3, base, pre, suf, table, weights,
    send1, recv1, send2, recv2, send3, recv3,
):
    s = lax.axis_index("slab")
    r = lax.axis_index("mode")
    barrier = pltpu.get_barrier_semaphore()

    def greet_mode(o, _):
        pl.semaphore_signal(barrier, 1, device_id={"mode": lax.rem(r + o, GROUP)})
        return 0

    def greet_slab(o, _):
        pl.semaphore_signal(barrier, 1, device_id={"slab": lax.rem(s + o, SLABS)})
        return 0

    lax.fori_loop(1, GROUP, greet_mode, 0)
    lax.fori_loop(1, SLABS, greet_slab, 0)

    box0, box1 = box[0], box[1]
    height = SPAN / SLABS
    lower = s.astype(F32) * height

    lane = iota((64, 128), 1)
    row = iota((64, 128), 0)
    order_p = (lane % 64 + 1).astype(F32)
    _, _, norm = waves(order_p, y_order(row), box0, box1)
    half = norm * (0.5 * height)
    decay = jnp.exp(-half)
    boost = jnp.exp(norm * height)
    power = decay
    for l in range(POWERS):
        tab[l] = power * EXP[l]
        power = power * half
    lane1 = iota((8, 128), 1)
    row1 = iota((8, 128), 0)
    p1 = (lane1 % 64 + 1).astype(F32)
    _, _, norm32 = waves(p1, jnp.full((8, 128), 32.0, F32), box0, box1)
    half32 = norm32 * (0.5 * height)
    power = jnp.exp(-half32)
    t32 = jnp.zeros((8, 128), F32)
    for l in range(POWERS):
        t32 = jnp.where(row1 == l, power * EXP[l], t32)
        power = power * half32
    tab32[...] = t32

    live = counts[s] - r * OWN
    slot = iota((1, OWN), 1)
    weights[...] = jnp.where(slot < live, chg[...], 0.0)
    sign = jnp.where(iota((1, 128), 1) < 64, -1.0, 1.0)

    def moments(b, _):
        ds = pl.ds(pl.multiple_of(b * BLOCK, BLOCK), BLOCK)
        x = pos[0:1, ds]
        y = pos[1:2, ds]
        w = weights[0:1, ds]
        u = (pos[2:3, ds] - lower) * (2.0 / height) - 1.0
        for g in range(4):
            p = (iota((16, BLOCK), 0) + (16 * g + 1)).astype(F32)
            t = frac(p * x)
            for half_row, v in ((0, cos_turn(t)), (64, sin_turn(t))):
                at = half_row + 16 * g
                e_ref[at : at + 16, ds] = v
                hi, lo = split(w * v)
                we[at : at + 16, :] = hi
                we[128 + at : 144 + at, :] = lo
        powers = [jnp.ones_like(u)]
        for l in range(1, POWERS):
            powers.append(powers[-1] * u)
        for g in range(4):
            t = frac(y_order(iota((16, BLOCK), 0) + 16 * g) * y)
            f = cos_turn(t) if g < 2 else sin_turn(t)
            for l in range(POWERS):
                at = 64 * l + 16 * g
                v = f * powers[l] if l else f
                if l < 3:
                    hi, lo = split(v)
                    tf[LOW + at : LOW + at + 16, ds] = lo
                else:
                    hi = v.astype(BF16)
                tf[at : at + 16, ds] = hi
        c32 = cos_turn(frac(32.0 * y))
        v = jnp.concatenate([c32 * q for q in powers], axis=0)
        hi = v.astype(BF16).astype(F32)
        tf[EXTRA : EXTRA + 16, ds] = jnp.concatenate([hi, hi], axis=0).astype(BF16)
        tf[EXTRA + 16 : EXTRA + 32, ds] = jnp.concatenate([v - hi, jnp.zeros_like(v)], axis=0).astype(BF16)
        tf[EXTRA + 32 : EXTRA + 64, ds] = jnp.zeros((32, BLOCK), BF16)

        stack[...] = lax.dot_general(
            tf[:, ds], we[...], (((1,), (1,)), ((), ())), preferred_element_type=F32
        )
        sides = []
        for first in (0, 1):
            acc = None
            acc32 = None
            for l in range(first, POWERS, 2):
                m = stack[64 * l : 64 * l + 64, 0:128] + stack[64 * l : 64 * l + 64, 128:256]
                if l < 3:
                    m = m + stack[LOW + 64 * l : LOW + 64 * l + 64, 0:128]
                acc = tab[l] * m if acc is None else acc + tab[l] * m
            sides.append(acc)
        m32 = stack[EXTRA : EXTRA + 8, 0:128] + stack[EXTRA : EXTRA + 8, 128:256] + stack[EXTRA + 16 : EXTRA + 24, 0:128]
        m32 = tab32[...] * m32
        even = jnp.sum(jnp.where(row1 % 2 == 0, m32, 0.0), axis=0, keepdims=True)
        odd = jnp.sum(jnp.where(row1 % 2 == 1, m32, 0.0), axis=0, keepdims=True)
        for ref, m, m_last in (
            (up, sides[0] + sides[1], even + odd),
            (down, sides[0] - sides[1], even - odd),
        ):
            fixed = 0.5 * (m[32:33] + sign * turn(m_last))
            ref[b] = jnp.where(row == 32, fixed, m)
        return 0

    lax.fori_loop(0, BLOCKS, moments, 0)

    sum_up = up[0]
    for b in range(1, BLOCKS):
        sum_up = sum_up + up[b]
    sum_down = down[0]
    for b in range(1, BLOCKS):
        sum_down = sum_down + down[b]
    total[:, 0] = sum_up.reshape(GROUP, 8, 128)
    total[:, 1] = sum_down.reshape(GROUP, 8, 128)
    rx1[r] = total[r]

    pl.semaphore_wait(barrier, GROUP - 1 + SLABS - 1)

    def copy1(j):
        return pltpu.make_async_remote_copy(
            total.at[j], rx1.at[r], send1.at[j], recv1.at[r], device_id={"mode": j}
        )

    def take1(j):
        return pltpu.make_async_remote_copy(
            total.at[j], rx1.at[j], send1.at[j], recv1.at[j], device_id={"mode": j}
        )

    def over_group(act):
        def step(o, _):
            act(lax.rem(r + o, GROUP))
            return 0

        lax.fori_loop(1, GROUP, step, 0)

    def over_slabs(act):
        def step(o, _):
            act(lax.rem(s + o, SLABS))
            return 0

        lax.fori_loop(1, SLABS, step, 0)

    over_group(lambda j: copy1(j).start())

    run = jnp.zeros((64, 128), F32)
    for b in range(BLOCKS):
        pre[b] = boost * run
        run = run + up[b]
    run = jnp.zeros((64, 128), F32)
    for b in range(BLOCKS - 1, -1, -1):
        suf[b] = boost * run
        run = run + down[b]

    over_group(lambda j: take1(j).wait())

    slab_up = rx1[0, 0]
    slab_down = rx1[0, 1]
    for j in range(1, GROUP):
        slab_up = slab_up + rx1[j, 0]
        slab_down = slab_down + rx1[j, 1]
    sums[0] = slab_up
    sums[1] = slab_down
    rx2[s] = jnp.zeros((8, 128), F32)

    def copy2(t, slot_at):
        return pltpu.make_async_remote_copy(
            sums.at[jnp.where(t < s, 1, 0)], rx2.at[slot_at], send2.at[t], recv2.at[slot_at], device_id={"slab": t}
        )

    over_slabs(lambda t: copy2(t, s).start())

    lane2 = iota((128, 128), 1)
    p2 = (iota((128, 128), 0) % 64 + 1).astype(F32)
    q2 = y_order(lane2 % 64)
    kx, ky, norm2 = waves(p2, q2, box0, box1)
    half2 = norm2 * (0.5 * height)
    scale = 2.0 * TWO_PI / (box0 * box1)
    common = scale * jnp.where(q2 == 0.0, 1.0, 2.0) * jnp.exp(-half2)
    square = half2 * half2
    odd_lane = lane2 >= 64
    power = jnp.where(odd_lane, half2, 1.0) * common
    ux = kx / norm2
    uy = ky / norm2
    for j in range(POWERS // 2):
        t = power * jnp.where(odd_lane, EXP[2 * j + 1], EXP[2 * j])
        table[0, j] = t * ux
        table[1, j] = t * uy
        table[2, j] = -t
        power = power * square
    kx32, ky32, _ = waves(p1, jnp.full((8, 128), 32.0, F32), box0, box1)
    base32 = (2.0 * scale) * t32
    x32 = base32 * (kx32 / norm32)
    y32 = -base32 * (ky32 / norm32)

    slice_row = 8 * r + row1
    _, _, norm_s = waves(p1, y_order(slice_row), box0, box1)
    step_s = norm_s * height
    boost_s = jnp.exp(step_s)
    run = jnp.zeros((8, 128), F32)
    for j in range(GROUP):
        tx3[j, 0] = boost_s * run
        run = run + rx1[j, 0]
    run = jnp.zeros((8, 128), F32)
    for j in range(GROUP - 1, -1, -1):
        tx3[j, 1] = boost_s * run
        run = run + rx1[j, 1]

    over_slabs(lambda t: copy2(t, t).wait())

    carry_up = jnp.zeros((8, 128), F32)
    carry_down = jnp.zeros((8, 128), F32)
    for t in range(SLABS):
        gap = jnp.maximum(jnp.abs(s - t) - 1, 0).astype(F32)
        term = jnp.exp(-step_s * gap) * rx2[t]
        carry_up = carry_up + jnp.where(t < s, term, 0.0)
        carry_down = carry_down + jnp.where(t > s, term, 0.0)
    for j in range(GROUP):
        tx3[j, 0] = tx3[j, 0] + carry_up
        tx3[j, 1] = tx3[j, 1] + carry_down
    base[r] = tx3[r]

    def copy3(j, slot_at):
        return pltpu.make_async_remote_copy(
            tx3.at[j], base.at[slot_at], send3.at[j], recv3.at[slot_at], device_id={"mode": j}
        )

    over_group(lambda j: copy3(j, r).start())
    over_group(lambda j: copy3(j, j).wait())

    parity = row1 % 2 == 0
    zeros8 = jnp.zeros((8, 128), F32)

    def forces(b, _):
        ds = pl.ds(pl.multiple_of(b * BLOCK, BLOCK), BLOCK)
        g_up = base[:, 0].reshape(64, 128) + pre[b]
        g_down = base[:, 1].reshape(64, 128) + suf[b]
        plus = g_up + g_down
        minus = g_down - g_up
        plus32 = -sign * turn(plus[32:33])
        minus32 = -sign * turn(minus[32:33])

        def swapped(g, g32):
            return jnp.where(row == 32, g32, jnp.concatenate([-g[32:64], g[0:32]], axis=0))

        straight = jnp.concatenate([plus, minus], axis=0).T
        crossed = jnp.concatenate([swapped(plus, plus32), swapped(minus, minus32)], axis=0).T
        sources = (straight, crossed, turn(straight))
        extras = (
            x32 * jnp.where(parity, plus32, minus32),
            y32 * jnp.where(parity, plus[32:33], minus[32:33]),
            -base32 * jnp.where(parity, minus32, plus32),
        )
        main_rows = []
        low_rows = []
        for f in range(3):
            his = []
            los = []
            for j in range(POWERS // 2):
                h = table[f, j] * sources[f]
                if j < 2:
                    hi, lo = split(h)
                    los.append(lo)
                else:
                    hi = h.astype(BF16)
                his.append(hi)
            v = extras[f]
            hi8 = v.astype(BF16).astype(F32)
            spread = jnp.concatenate(
                [jnp.zeros((64, 128), F32), hi8, v - hi8, hi8, jnp.zeros((40, 128), F32)], axis=0
            ).T
            last = jnp.where(lane2 < 64, table[f, 1] * sources[f], spread).astype(BF16)
            main_rows.append(jnp.concatenate(his + [his[0], last], axis=1))
            low_rows.append(jnp.concatenate(los, axis=1))
        mains = jnp.concatenate(main_rows, axis=0)
        lows = jnp.concatenate(low_rows, axis=0)
        product = lax.dot_general(mains, tf[:, ds], (((1,), (0,)), ((), ())), preferred_element_type=F32)
        product = product + lax.dot_general(
            lows, tf[0:256, ds], (((1,), (0,)), ((), ())), preferred_element_type=F32
        )
        w = weights[0:1, ds]
        cosine = e_ref[0:64, ds]
        sine = e_ref[64:128, ds]
        fx = jnp.sum(sine * product[0:64] - cosine * product[64:128], axis=0, keepdims=True)
        fy = jnp.sum(cosine * product[128:192] + sine * product[192:256], axis=0, keepdims=True)
        fz = jnp.sum(cosine * product[256:320] + sine * product[320:384], axis=0, keepdims=True)
        out[0:1, ds] = w * fx
        out[1:2, ds] = w * fy
        out[2:3, ds] = w * fz
        return 0

    lax.fori_loop(0, BLOCKS, forces, 0)


def shards(positions, charges, counts, box):
    vmem = pl.BlockSpec(memory_space=pltpu.VMEM)
    smem = pl.BlockSpec(memory_space=pltpu.SMEM)
    tile = (8, 128)
    return pl.pallas_call(
        kernel,
        out_shape=jax.ShapeDtypeStruct((3, OWN), F32),
        in_specs=[smem, smem, vmem, vmem],
        out_specs=vmem,
        scratch_shapes=[
            pltpu.VMEM((ROWS, OWN), BF16),
            pltpu.VMEM((128, OWN), F32),
            pltpu.VMEM((256, BLOCK), BF16),
            pltpu.VMEM((ROWS, 256), F32),
            pltpu.VMEM((POWERS, 64, 128), F32),
            pltpu.VMEM(tile, F32),
            pltpu.VMEM((BLOCKS, 64, 128), F32),
            pltpu.VMEM((BLOCKS, 64, 128), F32),
            pltpu.VMEM((GROUP, 2) + tile, F32),
            pltpu.VMEM((GROUP, 2) + tile, F32),
            pltpu.VMEM((2,) + tile, F32),
            pltpu.VMEM((SLABS,) + tile, F32),
            pltpu.VMEM((GROUP, 2) + tile, F32),
            pltpu.VMEM((GROUP, 2) + tile, F32),
            pltpu.VMEM((BLOCKS, 64, 128), F32),
            pltpu.VMEM((BLOCKS, 64, 128), F32),
            pltpu.VMEM((3, POWERS // 2, 128, 128), F32),
            pltpu.VMEM((1, OWN), F32),
            pltpu.SemaphoreType.DMA((GROUP,)),
            pltpu.SemaphoreType.DMA((GROUP,)),
            pltpu.SemaphoreType.DMA((SLABS,)),
            pltpu.SemaphoreType.DMA((SLABS,)),
            pltpu.SemaphoreType.DMA((GROUP,)),
            pltpu.SemaphoreType.DMA((GROUP,)),
        ],
        compiler_params=pltpu.CompilerParams(collective_id=0, has_side_effects=True),
    )(counts, box, positions, charges.reshape(1, OWN))


def solution(mesh):
    return jax.shard_map(
        shards,
        mesh=mesh,
        in_specs=(P(None, ("slab", "mode")), P(("slab", "mode")), P(), P()),
        out_specs=P(None, ("slab", "mode")),
        check_vma=False,
    )
```

time: 588 us -> 31.8 us (0.05)
  other arithmetic: 343 us -> 0 us
  blocking collectives: 132 us -> 0 us
  waiting for transfers between devices: 82.8 us -> 0 us
  Pallas kernels: 0 us -> 30.2 us
  between operations: 14.9 us -> 0.01 us
  local copies, waits for them, and re-layouts: 11.1 us -> 1.38 us
    reduce_sum x18 -> x0, other arithmetic: 168 us -> none  [the longest x8 155 us: force_terms(): jnp.sum(unit_x[:, None] * in_plane, axis=0)]
    mul x16 -> x0, other arithmetic: 138 us -> none  [the longest x8 137 us: block_moments(): upward * cosine]
    all_gather x5 -> x0, blocking collectives: 132 us -> none  [the longest x3 103 us: carried_in(): everything = jax.tree.map(lambda part: lax.all_gather(part, axis), value)]
    unnamed x2 -> x0, waiting for transfers between devices: 82.8 us -> none
    pallas_call x0 -> x1, Pallas kernels: none -> 30.2 us  [shards(): pl.pallas_call(kernel, out_shape=jax.ShapeDtypeStruct((3, OWN), F32), in_...]
    neg x16 -> x0, other arithmetic: 20.6 us -> none  [phase_terms(): e_high = jnp.exp(-wave_norm[:, None] * (height - ion_depth))]
    div x8 -> x0, other arithmetic: 10.2 us -> none  [wave_table(): return (order_p, order_q, wave_x / wave_norm, wave_y / wave_norm, wave_norm)]
  transfers between devices with their start and end apart: 1 -> 0, of which waited for: 1 -> 0; matrix products, arithmetic and copies ran while one was open for 0% -> 0% of each run, Pallas kernels for 0% -> 0%
where the time goes in v1:
time: 31.8 us; the launch traced here: 31.6 us
  Pallas kernels  30.2 us (95%)
  local copies, waits for them, and re-layouts  1.38 us (4%)
    pallas_call x1, Pallas kernels, shards(): pl.pallas_call(kernel, out_shape=jax.ShapeDtypeStruct((3, OWN), F32), in_...  30.2 us
    unnamed x1, local copies, waits for them, and re-layouts  1.38 us

profile of v1, /device:TPU:1, one launch (start us, length us, event | category | flops | bytes accessed | tf_op | source)
XLA Modules:
  0.0 31.6 jit_solution(12931931989585644892)
XLA Ops:
  0.0 30.2 %shard_map.46 = f32[3,2048]{1,0:T(4,128)} custom-call(s32[32]{0:T(128)} %counts.1, f32[2]{0:T(128)} %box.1, f32[3,2048]{1,0:T(4,128)} %pos.1, f32[1,2048]{1,0:T(1,128)} %bitcast.1), custom_call_target="tpu_custom_call" | custom-call | tf_op jit(solution)/shard_map/pallas_call | solution.py:389
  30.2 1.4 %copy.6 = f32[3,2048]{1,0:T(4,128)} copy(f32[3,2048]{1,0:T(4,128)} %shard_map.46) | data formatting | bytes 49152

commit v2 on v1

v2 whole, which is shorter than its diff:
```python
import math

import jax
import jax.numpy as jnp
from jax import lax
from jax.experimental import pallas as pl
from jax.experimental.pallas import tpu as pltpu
from jax.sharding import PartitionSpec as P

BLOCK = 512
SLABS = 32
GROUP = 8
OWN = 2048
BLOCKS = OWN // BLOCK
SPAN = 0.08
TWO_PI = 2.0 * math.pi
F32 = jnp.float32
BF16 = jnp.bfloat16

EXP = (
    0.999999988350913, 0.9999999941834263, 0.5000007545561663, 0.16666682366413116,
    0.04165903378572252, 0.008332189708132568, 0.001413565070950797, 0.0002014945763397459,
)
COS = (
    0.9999999890590228, -19.73920449945383, 64.93911745989081, -85.45013953079767,
    60.167630950263465, -25.967599245923743, 6.52865815775625,
)
SIN = (
    6.283185302511503, -41.34170040531721, 81.6051313857832, -76.70301535364747,
    42.02592698447418, -14.899846663536497, 3.2381375046186873,
)
POWERS = 8

LOW = 64 * POWERS
EXTRA = LOW + 64 * 3
ROWS = EXTRA + 64


def horner(coefs, z):
    acc = coefs[-1] * z + coefs[-2]
    for c in coefs[-3::-1]:
        acc = acc * z + c
    return acc


def frac(t):
    return t - jnp.round(t)


def cos_turn(r):
    return horner(COS, r * r)


def sin_turn(r):
    return r * horner(SIN, r * r)


def iota(shape, dim):
    return lax.broadcasted_iota(jnp.int32, shape, dim)


def split(v):
    hi = v.astype(BF16)
    return hi, (v - hi.astype(F32)).astype(BF16)


def y_order(index):
    order = jnp.where(index < 32, index, jnp.where(index == 32, 32, index - 32))
    return order.astype(F32)


def waves(order_p, order_q, box0, box1):
    wave_x = TWO_PI * order_p / box0
    wave_y = TWO_PI * order_q / box1
    return wave_x, wave_y, jnp.sqrt(wave_x * wave_x + wave_y * wave_y)


def turn(row):
    return pltpu.roll(row, 64, 1)


def hop_key(offset, size):
    return min(offset, size - offset)


GROUP_OFFSETS = sorted(
    ((dx, dc) for dx in range(4) for dc in range(2) if dx or dc), key=lambda o: -(2 * hop_key(o[0], 4) + o[1])
)
SLAB_OFFSETS = sorted(
    ((dy, dz) for dy in range(4) for dz in range(8) if dy or dz), key=lambda o: -(hop_key(o[0], 4) + hop_key(o[1], 8))
)


def kernel(
    counts_h, box_h, pos_h, chg_h, out,
    counts, box, pos, chg,
    tf, e_ref, we, stack, tab, up, down, total, rx1, sums, rx2, tx3, base, pre, suf, table, weights, decays, ht, part,
    load, ready, send1, recv1, send2, recv2, send3, recv3,
):
    s = lax.axis_index("slab")
    r = lax.axis_index("mode")
    at_y, at_z = s // 8, s % 8
    at_x, core = r // 2, r % 2

    def mate(offset):
        return lax.rem(at_x + offset[0], 4) * 2 + lax.rem(core + offset[1], 2)

    def slab_at(offset):
        return lax.rem(at_y + offset[0], 4) * 8 + lax.rem(at_z + offset[1], 8)

    barrier = pltpu.get_barrier_semaphore()
    lines = [o for o in SLAB_OFFSETS if o[0] == 0 or o[1] == 0]
    y_line = [o for o in SLAB_OFFSETS if o[1] == 0]
    for o in lines:
        pl.semaphore_signal(barrier, 1, device_id={"slab": slab_at(o)})
    for o in GROUP_OFFSETS:
        pl.semaphore_signal(barrier, 1, device_id={"mode": mate(o)})
    loads = [
        pltpu.make_async_copy(src, dst, load.at[i])
        for i, (src, dst) in enumerate(((pos_h, pos), (chg_h, chg), (counts_h, counts), (box_h, box)))
    ]
    for c in loads:
        c.start()
    height = SPAN / SLABS
    lower = s.astype(F32) * height
    lane = iota((64, 128), 1)
    row = iota((64, 128), 0)
    lane1 = iota((8, 128), 1)
    row1 = iota((8, 128), 0)
    p1 = (lane1 % 64 + 1).astype(F32)
    sign = jnp.where(iota((1, 128), 1) < 64, -1.0, 1.0)
    for c in loads:
        c.wait()
    box0, box1 = box[0], box[1]

    order_p = (lane % 64 + 1).astype(F32)
    _, _, norm = waves(order_p, y_order(row), box0, box1)
    half = norm * (0.5 * height)
    power = jnp.exp(-half)
    for l in range(POWERS):
        tab[l] = power * EXP[l]
        power = power * half
    _, _, norm32 = waves(p1, jnp.full((8, 128), 32.0, F32), box0, box1)
    half32 = norm32 * (0.5 * height)
    power = jnp.exp(-half32)
    t32 = jnp.zeros((8, 128), F32)
    for l in range(POWERS):
        t32 = jnp.where(row1 == l, power * EXP[l], t32)
        power = power * half32

    live = counts[s] - r * OWN
    slot = iota((1, OWN), 1)
    weights[...] = jnp.where(slot < live, chg[...], 0.0)

    def functions(b):
        ds = pl.ds(b * BLOCK, BLOCK)
        x = pos[0:1, ds]
        y = pos[1:2, ds]
        w = weights[0:1, ds]
        u = (pos[2:3, ds] - lower) * (2.0 / height) - 1.0
        for g in range(4):
            p = (iota((16, BLOCK), 0) + (16 * g + 1)).astype(F32)
            t = frac(p * x)
            for half_row, v in ((0, cos_turn(t)), (64, sin_turn(t))):
                at = half_row + 16 * g
                e_ref[at : at + 16, ds] = v
                hi, lo = split(w * v)
                we[b % 2, at : at + 16, :] = hi
                we[b % 2, 128 + at : 144 + at, :] = lo
        powers = [jnp.ones_like(u)]
        for l in range(1, POWERS):
            powers.append(powers[-1] * u)
        for g in range(4):
            t = frac(y_order(iota((16, BLOCK), 0) + 16 * g) * y)
            f = cos_turn(t) if g < 2 else sin_turn(t)
            for l in range(POWERS):
                at = 64 * l + 16 * g
                v = f * powers[l] if l else f
                if l < 3:
                    hi, lo = split(v)
                    tf[LOW + at : LOW + at + 16, ds] = lo
                else:
                    hi = v.astype(BF16)
                tf[at : at + 16, ds] = hi
        c32 = cos_turn(frac(32.0 * y))
        v = jnp.concatenate([c32 * q for q in powers], axis=0)
        hi = v.astype(BF16).astype(F32)
        tf[EXTRA : EXTRA + 16, ds] = jnp.concatenate([hi, hi], axis=0).astype(BF16)
        tf[EXTRA + 16 : EXTRA + 32, ds] = jnp.concatenate([v - hi, jnp.zeros_like(v)], axis=0).astype(BF16)
        tf[EXTRA + 32 : EXTRA + 64, ds] = jnp.zeros((32, BLOCK), BF16)

    def products(b):
        stack[b % 2] = lax.dot_general(
            tf[:, pl.ds(b * BLOCK, BLOCK)], we[b % 2], (((1,), (1,)), ((), ())), preferred_element_type=F32
        )

    def moments(b):
        m_of = stack.at[b % 2]
        sides = []
        for first in (0, 1):
            acc = None
            for l in range(first, POWERS, 2):
                m = m_of[64 * l : 64 * l + 64, 0:128] + m_of[64 * l : 64 * l + 64, 128:256]
                if l < 3:
                    m = m + m_of[LOW + 64 * l : LOW + 64 * l + 64, 0:128]
                acc = tab[l] * m if acc is None else acc + tab[l] * m
            sides.append(acc)
        m32 = m_of[EXTRA : EXTRA + 8, 0:128] + m_of[EXTRA : EXTRA + 8, 128:256] + m_of[EXTRA + 16 : EXTRA + 24, 0:128]
        m32 = t32 * m32
        even = jnp.sum(jnp.where(row1 % 2 == 0, m32, 0.0), axis=0, keepdims=True)
        odd = jnp.sum(jnp.where(row1 % 2 == 1, m32, 0.0), axis=0, keepdims=True)
        for ref, m, m_last in (
            (up, sides[0] + sides[1], even + odd),
            (down, sides[0] - sides[1], even - odd),
        ):
            fixed = 0.5 * (m[32:33] + sign * turn(m_last))
            ref[b] = jnp.where(row == 32, fixed, m)

    for b in range(BLOCKS):
        functions(b)
        products(b)
        moments(b)

    for side, ref in enumerate((up, down)):
        whole = (ref[0] + ref[1]) + (ref[2] + ref[3])
        total[:, side] = whole.reshape(GROUP, 8, 128)

    pl.semaphore_wait(barrier, len(lines) + len(GROUP_OFFSETS))
    for o in GROUP_OFFSETS:
        j = mate(o)
        pltpu.make_async_remote_copy(total.at[j], rx1.at[r], send1, recv1, device_id={"mode": j}).start()
    for o in y_line:
        pl.semaphore_signal(ready, 1, device_id={"slab": slab_at(o)})
    rx1[r] = total[r]

    boost = jnp.exp(norm * height)
    run = jnp.zeros((64, 128), F32)
    for b in range(BLOCKS):
        pre[b] = boost * run
        run = run + up[b]
    run = jnp.zeros((64, 128), F32)
    for b in range(BLOCKS - 1, -1, -1):
        suf[b] = boost * run
        run = run + down[b]

    lane2 = iota((128, 128), 1)
    p2 = (iota((128, 128), 0) % 64 + 1).astype(F32)
    q2 = y_order(lane2 % 64)
    kx, ky, norm2 = waves(p2, q2, box0, box1)
    half2 = norm2 * (0.5 * height)
    scale = 2.0 * TWO_PI / (box0 * box1)
    common = scale * jnp.where(q2 == 0.0, 1.0, 2.0) * jnp.exp(-half2)
    square = half2 * half2
    odd_lane = lane2 >= 64
    power = jnp.where(odd_lane, half2, 1.0) * common
    ux = kx / norm2
    uy = ky / norm2
    for j in range(POWERS // 2):
        t = power * jnp.where(odd_lane, EXP[2 * j + 1], EXP[2 * j])
        table[0, j] = t * ux
        table[1, j] = t * uy
        table[2, j] = -t
        power = power * square
    kx32, ky32, _ = waves(p1, jnp.full((8, 128), 32.0, F32), box0, box1)
    base32 = (2.0 * scale) * t32
    x32 = base32 * (kx32 / norm32)
    y32 = -base32 * (ky32 / norm32)
    parity = row1 % 2 == 0

    _, _, norm_s = waves(p1, y_order(8 * r + row1), box0, box1)
    step_s = norm_s * height
    boost_s = jnp.exp(step_s)
    for t in range(SLABS):
        gap = jnp.maximum(jnp.abs(s - t) - 1, 0).astype(F32)
        term = jnp.exp(-step_s * gap)
        decays[0, t] = jnp.where(t < s, term, 0.0)
        decays[1, t] = jnp.where(t > s, term, 0.0)
    rx2[s] = jnp.zeros((8, 128), F32)

    def weave(g_up, g_down):
        plus = g_up + g_down
        minus = g_down - g_up
        plus32 = -sign * turn(plus[32:33])
        minus32 = -sign * turn(minus[32:33])

        def swapped(g, g32):
            return jnp.where(row == 32, g32, jnp.concatenate([-g[32:64], g[0:32]], axis=0))

        straight = jnp.concatenate([plus, minus], axis=0).T
        crossed = jnp.concatenate([swapped(plus, plus32), swapped(minus, minus32)], axis=0).T
        sources = (straight, crossed, turn(straight))
        extras = (
            x32 * jnp.where(parity, plus32, minus32),
            y32 * jnp.where(parity, plus[32:33], minus[32:33]),
            -base32 * jnp.where(parity, minus32, plus32),
        )
        for f in range(3):
            rows = pl.ds(128 * f, 128)
            for j in range(POWERS // 2):
                h = table[f, j] * sources[f]
                if j < 2:
                    hi, lo = split(h)
                    ht[rows, 768 + 128 * j : 896 + 128 * j] = lo
                else:
                    hi = h.astype(BF16)
                ht[rows, 128 * j : 128 * j + 128] = hi
                if j == 0:
                    ht[rows, 512:640] = hi
            v = extras[f]
            hi8 = v.astype(BF16).astype(F32)
            spread = jnp.concatenate(
                [jnp.zeros((64, 128), F32), hi8, v - hi8, hi8, jnp.zeros((40, 128), F32)], axis=0
            ).T
            ht[rows, 640:768] = jnp.where(lane2 < 64, table[f, 1] * sources[f], spread).astype(BF16)

    def pull(b):
        ds = pl.ds(b * BLOCK, BLOCK)
        product = lax.dot_general(
            ht[:, 0:768], tf[:, ds], (((1,), (0,)), ((), ())), preferred_element_type=F32
        ) + lax.dot_general(
            ht[:, 768:1024], tf[0:256, ds], (((1,), (0,)), ((), ())), preferred_element_type=F32
        )
        cosine = e_ref[0:64, ds]
        sine = e_ref[64:128, ds]
        fx = jnp.sum(sine * product[0:64] - cosine * product[64:128], axis=0, keepdims=True)
        fy = jnp.sum(cosine * product[128:192] + sine * product[192:256], axis=0, keepdims=True)
        fz = jnp.sum(cosine * product[256:320] + sine * product[320:384], axis=0, keepdims=True)
        return jnp.concatenate([fx, fy, fz], axis=0)

    def local(b):
        weave(pre[b], suf[b])
        part[:, pl.ds(b * BLOCK, BLOCK)] = pull(b)

    local(0)
    local(1)

    pltpu.make_async_copy(rx1.at[0:7], rx1.at[0:7], recv1).wait()

    slab_up = rx1[0, 0]
    slab_down = rx1[0, 1]
    for j in range(1, GROUP):
        slab_up = slab_up + rx1[j, 0]
        slab_down = slab_down + rx1[j, 1]
    sums[0] = slab_up
    sums[1] = slab_down

    pl.semaphore_wait(ready, len(y_line))
    for o in SLAB_OFFSETS:
        t = slab_at(o)
        pltpu.make_async_remote_copy(
            sums.at[jnp.where(t < s, 1, 0)], rx2.at[s], send2, recv2, device_id={"slab": t}
        ).start()

    run = jnp.zeros((8, 128), F32)
    for j in range(GROUP):
        tx3[j, 0] = boost_s * run
        run = run + rx1[j, 0]
    run = jnp.zeros((8, 128), F32)
    for j in range(GROUP - 1, -1, -1):
        tx3[j, 1] = boost_s * run
        run = run + rx1[j, 1]
    local(2)
    local(3)

    pltpu.make_async_copy(rx2.at[0:31], rx2.at[0:31], recv2).wait()

    for side in range(2):
        terms = [decays[side, t] * rx2[t] for t in range(SLABS)]
        while len(terms) > 1:
            terms = [terms[i] + terms[i + 1] for i in range(0, len(terms), 2)]
        for j in range(GROUP):
            tx3[j, side] = tx3[j, side] + terms[0]

    for o in GROUP_OFFSETS:
        j = mate(o)
        pltpu.make_async_remote_copy(tx3.at[j], base.at[r], send3, recv3, device_id={"mode": j}).start()
    base[r] = tx3[r]
    pltpu.make_async_copy(base.at[0:7], base.at[0:7], recv3).wait()

    weave(base[:, 0].reshape(64, 128), base[:, 1].reshape(64, 128))
    for b in range(BLOCKS):
        ds = pl.ds(b * BLOCK, BLOCK)
        out[:, ds] = weights[0:1, ds] * (part[:, ds] + pull(b))

    pltpu.make_async_copy(total.at[0:7], total.at[0:7], send1).wait()
    pltpu.make_async_copy(rx2.at[0:31], rx2.at[0:31], send2).wait()
    pltpu.make_async_copy(tx3.at[0:7], tx3.at[0:7], send3).wait()


def shards(positions, charges, counts, box):
    vmem = pl.BlockSpec(memory_space=pltpu.VMEM)
    anywhere = pl.BlockSpec(memory_space=pl.ANY)
    tile = (8, 128)
    return pl.pallas_call(
        kernel,
        out_shape=jax.ShapeDtypeStruct((3, OWN), F32),
        in_specs=[anywhere] * 4,
        out_specs=vmem,
        scratch_shapes=[
            pltpu.SMEM((SLABS,), jnp.int32),
            pltpu.SMEM((2,), F32),
            pltpu.VMEM((3, OWN), F32),
            pltpu.VMEM((1, OWN), F32),
            pltpu.VMEM((ROWS, OWN), BF16),
            pltpu.VMEM((128, OWN), F32),
            pltpu.VMEM((2, 256, BLOCK), BF16),
            pltpu.VMEM((2, ROWS, 256), F32),
            pltpu.VMEM((POWERS, 64, 128), F32),
            pltpu.VMEM((BLOCKS, 64, 128), F32),
            pltpu.VMEM((BLOCKS, 64, 128), F32),
            pltpu.VMEM((GROUP, 2) + tile, F32),
            pltpu.VMEM((GROUP, 2) + tile, F32),
            pltpu.VMEM((2,) + tile, F32),
            pltpu.VMEM((SLABS,) + tile, F32),
            pltpu.VMEM((GROUP, 2) + tile, F32),
            pltpu.VMEM((GROUP, 2) + tile, F32),
            pltpu.VMEM((BLOCKS, 64, 128), F32),
            pltpu.VMEM((BLOCKS, 64, 128), F32),
            pltpu.VMEM((3, POWERS // 2, 128, 128), F32),
            pltpu.VMEM((1, OWN), F32),
            pltpu.VMEM((2, SLABS) + tile, F32),
            pltpu.VMEM((384, 1024), BF16),
            pltpu.VMEM((3, OWN), F32),
            pltpu.SemaphoreType.DMA((4,)),
            pltpu.SemaphoreType.REGULAR,
            pltpu.SemaphoreType.DMA,
            pltpu.SemaphoreType.DMA,
            pltpu.SemaphoreType.DMA,
            pltpu.SemaphoreType.DMA,
            pltpu.SemaphoreType.DMA,
            pltpu.SemaphoreType.DMA,
        ],
        compiler_params=pltpu.CompilerParams(collective_id=0, has_side_effects=True),
    )(counts, box, positions, charges.reshape(1, OWN))


def solution(mesh):
    return jax.shard_map(
        shards,
        mesh=mesh,
        in_specs=(P(None, ("slab", "mode")), P(("slab", "mode")), P(), P()),
        out_specs=P(None, ("slab", "mode")),
        check_vma=False,
    )
```

time: 31.8 us -> 27.7 us (0.87)
  Pallas kernels: 30.2 us -> 26.1 us
    pallas_call x1, Pallas kernels: 30.2 us -> 26.1 us  [shards(): pl.pallas_call(kernel, out_shape=jax.ShapeDtypeStruct((3, OWN), F32), in_...]
where the time goes in v2:
time: 27.7 us; the launch traced here: 27.5 us
  Pallas kernels  26.1 us (94%)
  local copies, waits for them, and re-layouts  1.38 us (5%)
    pallas_call x1, Pallas kernels, shards(): pl.pallas_call(kernel, out_shape=jax.ShapeDtypeStruct((3, OWN), F32), in_...  26.1 us
    unnamed x1, local copies, waits for them, and re-layouts  1.38 us

profile of v2, /device:TPU:1, one launch (start us, length us, event | category | flops | bytes accessed | tf_op | source)
XLA Modules:
  0.0 27.5 jit_solution(148834958090094784)
XLA Ops:
  0.0 26.1 %shard_map.46 = f32[3,2048]{1,0:T(4,128)} custom-call(s32[32]{0:T(128)} %counts_h.1, f32[2]{0:T(128)} %box_h.1, f32[3,2048]{1,0:T(4,128)} %pos_h.1, f32[1,2048]{1,0:T(1,128)} %bitcast.1), custom_call_target="tpu_custom_call" | custom-call | tf_op jit(solution)/shard_map/pallas_call | solution.py:394
  26.1 1.4 %copy.6 = f32[3,2048]{1,0:T(4,128)} copy(f32[3,2048]{1,0:T(4,128)} %shard_map.46) | data formatting | bytes 49152

commit v3 on v2

--- a/solution.py
+++ b/solution.py
@@ -393,7 +393,7 @@
     tile = (8, 128)
     return pl.pallas_call(
         kernel,
-        out_shape=jax.ShapeDtypeStruct((3, OWN), F32),
+        out_shape=pltpu.VMEM((3, OWN), F32),
         in_specs=[anywhere] * 4,
         out_specs=vmem,
         scratch_shapes=[

time: 27.7 us -> 26.2 us (0.946)
  local copies, waits for them, and re-layouts: 1.38 us -> 0.62 us
  Pallas kernels: 26.1 us -> 25.5 us
    unnamed x1, local copies, waits for them, and re-layouts: 1.38 us -> 0.62 us
    pallas_call x1, Pallas kernels: 26.1 us -> 25.5 us  [shards(): pl.pallas_call(kernel, out_shape=pltpu.VMEM((3, OWN), F32), in_specs=[any...]
where the time goes in v3:
time: 26.2 us; the launch traced here: 26.1 us
  Pallas kernels  25.5 us (97%)
  local copies, waits for them, and re-layouts  0.62 us (2%)
    pallas_call x1, Pallas kernels, shards(): pl.pallas_call(kernel, out_shape=pltpu.VMEM((3, OWN), F32), in_specs=[any...  25.5 us
    unnamed x1, local copies, waits for them, and re-layouts  0.62 us

profile of v3, /device:TPU:1, one launch (start us, length us, event | category | flops | bytes accessed | tf_op | source)
XLA Modules:
  0.0 26.1 jit_solution(8226790752967320897)
XLA Ops:
  0.0 25.5 %shard_map.46 = f32[3,2048]{1,0:T(4,128)S(1)} custom-call(s32[32]{0:T(128)} %counts_h.1, f32[2]{0:T(128)} %box_h.1, f32[3,2048]{1,0:T(4,128)} %pos_h.1, f32[1,2048]{1,0:T(1,128)} %bitcast.1), custom_call_target="tpu_custom_call" | custom-call | tf_op jit(solution)/shard_map/pallas_call | solution.py:394
  25.5 0.6 %copy.6 = f32[3,2048]{1,0:T(4,128)} copy(f32[3,2048]{1,0:T(4,128)S(1)} %shard_map.46) | data formatting | bytes 49152
